TPU v7x, 512 devices: a whole 4x8x8 slice. The times are simulated.
512 devices in a mesh: grp: 16 (over y, z_lo), feat: 32 (over x, z_hi, core).
Axes of the slice: x: 4, y: 8, z: 8 (z_hi: 4, z_lo: 2; z = z_hi * 2 + z_lo), core: 2. Of those that a mesh axis runs over, the one named last changes fastest.
Arguments:
- points: bfloat16 [131072, 32], P(('grp', 'feat')), may hold values from -6 to 6
- dual_weights: float32 [131072, 64], P(('grp', 'feat')), may hold values from -6 to 6
- velocity: float32 [131072, 64], P(('grp', 'feat')), may hold values from -1.75 to 1.75
- observed: float32 [131072], P(('grp', 'feat')), may hold values from -12 to 12
- noise_draws: float32 [131072, 64], P(('grp', 'feat')), may hold values from -3 to 3
- frequencies: bfloat16 [32, 16384], P(None, 'feat'), may hold values from -1.5 to 1.5
- phases: float32 [16384], P('feat'), may hold values from 0 to 6.2832
- prior_weights: bfloat16 [16384, 64], P('feat'), may hold values from -6 to 6
- batch_tiles: int32 [2, 16, 1], P(None, 'grp'), may hold values from 0 to 63, as said below
Outputs:
- new_duals: float32 [131072, 64], P(('grp', 'feat'))
- new_velocity: float32 [131072, 64], P(('grp', 'feat'))
Inputs may be any that keep to these rules, and one draw needn't show every extreme that they name: `batch_tiles`: in each step the 1 tile numbers of a group are distinct.
All inputs are finite; a program needn't handle non-finite values.
Results may differ from a plain program's by a relative error of at most 0.0012.
Values may be sent and summed in bfloat16 or wider, within the bound.
A program may use at most 64 MiB of HBM per device.

v0:
```python
import math

import jax
import jax.numpy as jnp
from jax import lax
from jax.sharding import PartitionSpec as P

RFF = 16384
TILE = 128
TILES_G = 1
STEPS = 2


amplitude = 4.0
signal = 2.0
momentum = 0.9
step_size = 0.5


def kernel_values(picked, point_block, norm_block):
    row_sq = jnp.sum(jnp.square(picked.astype(jnp.float32)), axis=1)
    inner_prod = lax.dot_general(
        picked, point_block, (((1,), (1,)), ((), ())), preferred_element_type=jnp.float32
    )
    distance = row_sq[:, None] + norm_block[None, :] - 2.0 * inner_prod
    return (amplitude * jnp.exp(-distance / point_block.shape[1])).astype(jnp.bfloat16)


def kernel_block(picked, points, local_sq, duals_bf):
    total_rows = picked.shape[0]
    block_rows = math.gcd(total_rows, 1024)
    blocks = picked.reshape(total_rows // block_rows, block_rows, picked.shape[1])

    def one_block(part_rows):
        kernel_tile = kernel_values(part_rows, points, local_sq)
        return jnp.dot(kernel_tile, duals_bf, preferred_element_type=jnp.float32)

    return lax.map(one_block, blocks).reshape(total_rows, duals_bf.shape[1])


def tile_layout(tile_ids, tiles_per, feat_index):
    owner_rank = tile_ids // tiles_per
    offsets = (tile_ids % tiles_per)[:, None] * TILE + jnp.arange(TILE, dtype=jnp.int32)[None, :]
    owned_mask = jnp.broadcast_to((owner_rank == feat_index)[:, None], offsets.shape)
    return (offsets.reshape(-1), owned_mask.reshape(-1))


def masked_rows(points, offsets, owned_mask):
    picked = points[offsets].astype(jnp.float32)
    return jnp.where(owned_mask[:, None], picked, 0.0)


def local(
    points,
    dual_weights,
    velocity,
    observed,
    noise_draws,
    frequencies,
    phases,
    prior_weights,
    batch_tiles,
):
    group_count = lax.axis_size("grp")
    feat_count = lax.axis_size("feat")
    feat_index = lax.axis_index("feat")
    group_index = lax.axis_index("grp")
    local_points = points.shape[0]
    tiles_per = local_points // TILE
    group_rows = TILES_G * TILE
    inv_root = 1.0 / math.sqrt(local_points * group_count * feat_count)
    prior_scale = signal * math.sqrt(2.0 / RFF)
    local_sq = jnp.sum(jnp.square(points.astype(jnp.float32)), axis=1)
    layouts = [
        tile_layout(batch_tiles[step_index, 0], tiles_per, feat_index)
        for step_index in range(STEPS)
    ]
    for step_index in range(STEPS):
        offsets, owned_mask = layouts[step_index]
        batch_local = lax.psum(
            masked_rows(points, offsets, owned_mask).astype(jnp.bfloat16), "feat"
        )
        duals_bf = dual_weights.astype(jnp.bfloat16)
        phase_arg = (
            jnp.dot(batch_local, frequencies, preferred_element_type=jnp.float32) + phases[None, :]
        )
        features = jnp.cos(phase_arg).astype(jnp.bfloat16)
        prior_part = (
            jnp.dot(features, prior_weights, preferred_element_type=jnp.float32) * prior_scale
        )
        partial_sums = kernel_block(
            lax.all_gather(batch_local, "grp", axis=0, tiled=True), points, local_sq, duals_bf
        )
        summed = lax.psum(partial_sums, ("grp", "feat"))
        prior_vals = lax.psum(prior_part, "feat")
        combined = (
            lax.dynamic_slice_in_dim(summed, group_index * group_rows, group_rows, 0) * inv_root
            + prior_vals
        )
        gradient = combined - observed[offsets][:, None] + noise_draws[offsets]
        new_vel = momentum * velocity[offsets] - step_size * gradient
        new_duals = dual_weights[offsets] + new_vel
        target_rows = jnp.where(owned_mask, offsets, local_points)
        dual_weights = dual_weights.at[target_rows].set(new_duals, mode="drop")
        velocity = velocity.at[target_rows].set(new_vel, mode="drop")
    return (dual_weights, velocity)


def solution(mesh):
    return jax.shard_map(
        local,
        mesh=mesh,
        in_specs=(
            P(("grp", "feat"), None),
            P(("grp", "feat"), None),
            P(("grp", "feat"), None),
            P(("grp", "feat")),
            P(("grp", "feat"), None),
            P(None, "feat"),
            P("feat"),
            P("feat", None),
            P(None, "grp", None),
        ),
        out_specs=(P(("grp", "feat"), None), P(("grp", "feat"), None)),
        check_vma=False,
    )
```

profile of v0, /device:TPU:1, one launch (start us, length us, event | category | flops | bytes accessed | tf_op | source)
XLA Modules:
  0.0 986.2 jit_solution(4149236005081590035)
XLA Ops:
  7.2 1.3 fusion.62
  16.1 143.8 %all-reduce.1 = (bf16[128,32]{1,0:T(8,128)(2,1)S(1)}, bf16[128,32]{1,0:T(8,128)(2,1)S(1)}) all-reduce(bf16[128,32]{1,0:T(8,128)(2,1)S(1)} %select_convert_fusion.1, bf16[128,32]{1,0:T(8,128)(2,1)S(1)} %select_convert_fusion), channel_id=1, replica_groups=mesh['grp'=16,'feat'=32] {'feat'}, use_global_device_ids=true, to_apply=%region_0.0 | all-reduce | flops 8192 | bytes 32768 | tf_op jit(solution)/shard_map/psum | solution.py:80
  159.9 1.7 fusion.52
  161.6 1.7 fusion.53
  163.5 30.2 %all_gather.6 = bf16[2048,32]{1,0:T(8,128)(2,1)S(1)} all-gather(bf16[128,32]{1,0:T(8,128)(2,1)S(1)} %get-tuple-element.98), channel_id=1, replica_groups=mesh['grp'=16,'feat'=32] {'grp'}, dimensions={0}, use_global_device_ids=true | all-gather | bytes 139264 | tf_op jit(solution)/shard_map/all_gather | solution.py:92
  194.0 5.9 while.20
  195.0 1.9 dynamic_update_slice.9
  198.0 1.9 dynamic_update_slice.9
  199.9 1.0 copy.58
  203.3 1.3 gather_fusion.3
  205.4 26.8 %all_gather.7 = bf16[2048,32]{1,0:T(8,128)(2,1)S(1)} all-gather(bf16[128,32]{1,0:T(8,128)(2,1)S(1)} %get-tuple-element.99), channel_id=1, replica_groups=mesh['grp'=16,'feat'=32] {'grp'}, dimensions={0}, use_global_device_ids=true | all-gather | bytes 139264 | tf_op jit(solution)/shard_map/all_gather | solution.py:92
  232.2 190.2 %all-reduce.10.cloned.1.call-done = (f32[128,64]{0,1:T(8,128)}, f32[128,64]{0,1:T(8,128)}) async-done(((f32[128,64]{0,1:T(8,128)}, f32[128,64]{0,1:T(8,128)}), (f32[128,64]{0,1:T(8,128)}, f32[128,64]{0,1:T(8,128)})) %all-reduce.10.cloned.1.call-update) | async-done | bytes 65552 | tf_op jit(solution)/shard_map/psum | solution.py:95
  422.4 274.9 %all-reduce.6.cloned.1.call-done = f32[2048,64]{0,1:T(8,128)} async-done(((f32[2048,64]{0,1:T(8,128)}), f32[2048,64]{0,1:T(8,128)}) %all-reduce.6.cloned.1.call-update) | async-done | bytes 524304 | tf_op jit(solution)/shard_map/psum | solution.py:94
  697.3 0.8 fusion.61
  698.2 1.0 scatter_fusion
  699.3 5.9 while.21
  700.4 1.9 dynamic_update_slice.10
  703.3 1.9 dynamic_update_slice.10
  705.2 1.0 copy.59
  706.9 1.3 gather_fusion.8
  709.1 1.0 scatter_fusion.1
  710.7 264.6 %all-reduce.8.cloned.1.call-done = f32[2048,64]{0,1:T(8,128)} async-done(((f32[2048,64]{0,1:T(8,128)}), f32[2048,64]{0,1:T(8,128)}) %all-reduce.8.cloned.1.call-update) | async-done | bytes 524304 | tf_op jit(solution)/shard_map/psum | solution.py:94
  976.2 1.0 scatter_fusion.2
  978.0 1.0 scatter_fusion.3
  (72 shorter events, 14.8 us)
Async XLA Ops:
  7.2 152.7 %copy-start = (bf16[512,64]{0,1:T(8,128)(2,1)S(1)}, bf16[512,64]{0,1:T(8,128)(2,1)}, u32[]{:S(2)}) copy-start(bf16[512,64]{0,1:T(8,128)(2,1)} %param.20) | copy-start | bytes 196612
  7.2 415.3 %all-reduce.10.cloned.1.call-start = ((), (), s32[]{:S(2)}) async-start(), calls=%async_computation.2 | async-start | bytes 131072 | tf_op jit(solution)/shard_map/psum | solution.py:95
  13.8 0.7 copy-start.5
  16.1 143.8 %copy-start.7 = (bf16[32,512]{1,0:T(8,128)(2,1)S(1)}, bf16[32,512]{1,0:T(8,128)(2,1)}, u32[]{:S(2)}) copy-start(bf16[32,512]{1,0:T(8,128)(2,1)} %param.18) | copy-start | bytes 98308
  16.1 143.8 %copy-start.8 = (f32[512]{0:T(512)S(1)}, f32[512]{0:T(512)}, u32[]{:S(2)}) copy-start(f32[512]{0:T(512)} %param.19) | copy-start | bytes 6148
  163.4 30.3 %copy-start.2 = (f32[256,64]{0,1:T(8,128)S(1)}, f32[256,64]{0,1:T(8,128)}, u32[]{:S(2)}) copy-start(f32[256,64]{0,1:T(8,128)} %param.14) | copy-start | bytes 196612
  163.4 533.9 %all-reduce.6.cloned.1.call-start = ((), (), s32[]{:S(2)}) async-start(), calls=%async_computation | async-start | bytes 1048576 | tf_op jit(solution)/shard_map/psum | solution.py:94
  200.9 774.4 %all-reduce.8.cloned.1.call-start = ((), (), s32[]{:S(2)}) async-start(), calls=%async_computation.1 | async-start | bytes 1048576 | tf_op jit(solution)/shard_map/psum | solution.py:94
  201.6 0.8 copy-start.3
  202.5 0.7 copy-start.1
  203.3 1.3 copy-start.4
  710.7 264.7 %copy-start.6 = (f32[128,64]{0,1:T(8,128)S(1)}, f32[128,64]{0,1:T(8,128)}, u32[]{:S(2)}) copy-start(f32[128,64]{0,1:T(8,128)} %get-tuple-element.97) | copy-start | bytes 98308
Sparse Core Ops, SparseCore 0:
  163.5 258.8 all-reduce.9
  427.4 269.8 all-reduce.5
  706.4 268.9 all-reduce.7
where the time goes:
time: 987 us; the launch traced here: 986 us
  waiting for transfers between devices  730 us (74%)
  blocking collectives  201 us (20%)
  local copies, waits for them, and re-layouts  27.9 us (3%)
  between operations  19.2 us (2%)
    psum x2, waiting for transfers between devices, local(): summed = lax.psum(partial_sums, ('grp', 'feat'))  539 us
    psum x1, waiting for transfers between devices, local(): prior_vals = lax.psum(prior_part, 'feat')  190 us
    psum x1, blocking collectives, local(): lax.psum(masked_rows(points, offsets, owned_mask).astype(jnp.bfloat16), '...  144 us
    all_gather x2, blocking collectives, local(): lax.all_gather(batch_local, 'grp', axis=0, tiled=True)  57.1 us
  transfers between devices with their start and end apart: 3, of which 3 were waited for; matrix products, arithmetic and copies ran while one was open for 2% of the time, Pallas kernels for 0%

commit v1 on v0

v1 whole, which is shorter than its diff:
```python
import functools
import math

import jax
import jax.numpy as jnp
from jax import lax
from jax.experimental import pallas as pl
from jax.experimental.pallas import tpu as pltpu
from jax.sharding import PartitionSpec as P

TILE = 128
STEPS = 2
NX = 4
MESH = pl.DeviceIdType.MESH

amplitude = 4.0
signal = 2.0
momentum = 0.9
step_size = 0.5

F32 = jnp.float32
BF16 = jnp.bfloat16

PI_HI = 3.140625
PI_LO = 9.67653589793e-4
INV_TWO_PI = 0.15915494309189535


def cosine(arg):
    turns = jnp.floor(arg * INV_TWO_PI + 0.5)
    half = arg * 0.5 - turns * PI_HI
    half = half - turns * PI_LO
    sq = half * half
    poly = sq * 2.6000493542416553e-06 + -0.00019806612414667135
    poly = poly * sq + 0.0083330172462401
    poly = poly * sq + -0.16666657094222279
    sine = half + half * (sq * poly)
    return 1.0 - 2.0 * (sine * sine)


def dot00(a, b):
    return lax.dot_general(a, b, (((0,), (0,)), ((), ())), preferred_element_type=F32)


def dot11(a, b):
    return lax.dot_general(a, b, (((1,), (1,)), ((), ())), preferred_element_type=F32)


def dot10(a, b):
    return lax.dot_general(a, b, (((1,), (0,)), ((), ())), preferred_element_type=F32)


def split_norm(cols):
    wide = cols.astype(F32)
    norm = jnp.sum(wide * wide, axis=0, keepdims=True) * (-1.0 / cols.shape[0])
    hi = norm.astype(BF16).astype(F32)
    rest = norm - hi
    mid = rest.astype(BF16).astype(F32)
    return hi, mid, rest - mid


def extra_rows(terms, width, first):
    rows = lax.broadcasted_iota(jnp.int32, (16, width), 0)
    out = jnp.where((rows >= 3 - first) & (rows < 6 - first), 1.0, 0.0)
    for i in range(3):
        out = jnp.where(rows == first + i, terms[i], out)
    return out.astype(BF16)


def kernel(
    nx, ny, nz, total_points, total_feats,
    bt, pT, uT, vT, ob, nT, fr, ph, wT,
    ou, ov,
    gat, pa, xs1, xr1, xs2, xr2, xa, xy, pa0, kc,
    pf, pr, zs, zr, vg, vy, cs, co, fin, cr, ssem, rsem,
):
    nh = nz // 2
    ns = nx * 2
    g = lax.axis_index("grp")
    f = lax.axis_index("feat")
    y = lax.div(g, 2)
    zl = lax.rem(g, 2)
    x = lax.div(f, nh * 2)
    c = lax.rem(f, 2)
    zh = lax.rem(lax.div(f, 2), nh)
    z = zh * 2 + zl
    s = x * 2 + c

    def at(s_, y_, z_):
        return {
            "grp": y_ * 2 + lax.rem(z_, 2),
            "feat": lax.div(s_, 2) * (nh * 2) + lax.div(z_, 2) * 2 + lax.rem(s_, 2),
        }

    def far_first(n):
        return sorted(range(1, n), key=lambda k: -min(k, n - k))

    block_of = {j: lax.rem(s + j, ns) for j in range(1, ns)}
    s_order = sorted(range(1, ns), key=lambda j: (-min(j, ns - j), j))
    z_flip = zh * 2 + (1 - zl)
    s_dev = {j: at(block_of[j], y, z) for j in block_of}
    p_dev = {j: at(block_of[j], y, z_flip) for j in block_of}
    p_dev[0] = at(s, y, z_flip)
    y_dev = {k: at(s, lax.rem(y + k, ny), z) for k in range(1, ny)}
    z_dev = {k: at(s, y, lax.rem(z + k, nz)) for k in range(1, nz)}

    barrier = pltpu.get_barrier_semaphore()
    greeted = list(s_dev.values()) + list(y_dev.values()) + list(z_dev.values())
    greeted += [p_dev[j] for j in block_of]
    for d in greeted:
        pl.semaphore_signal(barrier, inc=1, device_id=d, device_id_type=MESH)

    started = []

    def send(src, dst, dev):
        i = len(started)
        copy = pltpu.make_async_remote_copy(
            src_ref=src, dst_ref=dst, send_sem=ssem.at[i], recv_sem=rsem.at[i],
            device_id=dev, device_id_type=MESH,
        )
        copy.start()
        started.append(copy)
        return copy

    def owned(t):
        tile = bt[t]
        return lax.div(tile, 2) == f, lax.rem(tile, 2) == 0

    def pick(ref, low):
        return jnp.where(low, ref[:, :TILE], ref[:, TILE:])

    gat[0, 0:32, :] = pT[...]
    gat[0, 32:96, :] = uT[...].astype(BF16)
    for t in range(STEPS):
        mine, low = owned(t)
        xs1[t] = jnp.where(mine, pick(pT, low).astype(F32), 0.0).astype(BF16)
    pl.semaphore_wait(barrier, len(greeted))

    hop_c = [[send(xs1.at[t], xr1.at[j, t], s_dev[j]) for j in s_order] for t in range(STEPS)]
    bulk = {k: send(gat.at[0], gat.at[k], y_dev[k]) for k in far_first(ny)}
    hop_d = []
    for t in range(STEPS):
        for copy in hop_c[t]:
            copy.wait_recv()
        acc = xs1[t]
        for j in range(1, ns):
            acc = acc + xr1[j, t]
        xs2[t] = acc
        hop_d.append([send(xs2.at[t], xr2.at[k, t], z_dev[k]) for k in far_first(nz)])

    def build_points(k):
        block = gat[k, 0:32, :]
        pa[k, 0:32, :] = block
        pa[k, 32:48, :] = extra_rows(split_norm(block), 2 * TILE, 3)

    def batch_rows(t):
        for copy in hop_d[t]:
            copy.wait_recv()
        own = xs2[t]
        for k in range(2, nz, 2):
            own = own + xr2[k, t]
        oth = xr2[1, t]
        for k in range(3, nz, 2):
            oth = oth + xr2[k, t]
        if t == 0:
            xy[0] = own
        for i, rows in enumerate((own, oth)):
            lanes = slice(i * TILE, (i + 1) * TILE)
            xa[t, 0:32, lanes] = (rows.astype(F32) * (2.0 / 32)).astype(BF16)
            xa[t, 32:48, lanes] = extra_rows(split_norm(rows), TILE, 0)
        return own

    kv_scale = -step_size * amplitude / math.sqrt(total_points)
    prior_scale = -step_size * signal * math.sqrt(2.0 / total_feats)

    def prior_part(rows):
        feats = cosine(dot00(rows, fr[...]) + ph[...]).astype(BF16)
        return dot11(wT[...], feats) * prior_scale

    def kernel_part(t):
        xat = xa[t]

        def one(k, acc):
            kern = jnp.exp(dot00(pa[k], xat)).astype(BF16)
            return acc + dot10(gat[k, 32:96, :], kern)

        return lax.fori_loop(0, ny, one, jnp.zeros((64, 2 * TILE), F32), unroll=True) * kv_scale

    def own_terms(t):
        mine, low = owned(t)
        terms = step_size * (pick(ob, low) - pick(nT, low))
        if t == 0:
            terms = terms + momentum * pick(vT, low)
        return jnp.where(mine, terms, 0.0)

    def partial(t, prior):
        part = kernel_part(t)
        own = part[:, :TILE] + prior + own_terms(t)
        pf[t, :, :, 0:TILE] = own.reshape(ns, 64 // ns, TILE)
        pf[t, :, :, TILE:] = part[:, TILE:].reshape(ns, 64 // ns, TILE)
        return [send(pf.at[t, block_of[j]], pr.at[t, j], s_dev[j]) for j in s_order]

    def stage_z(t, hops):
        for copy in hops:
            copy.wait_recv()
        share = pf[t, s]
        for j in range(1, ns):
            share = share + pr[t, j]
        zs[t, 0] = share[:, :TILE]
        zs[t, 1] = share[:, TILE:]
        return [send(zs.at[t, k % 2], zr.at[t, k], z_dev[k]) for k in far_first(nz)]

    def stage_end(t, hops):
        for copy in hops:
            copy.wait_recv()
        share = zs[t, 0]
        for k in range(1, nz):
            share = share + zr[t, k]
        return share

    build_points(0)
    rows0 = batch_rows(0)
    hop_xy = [send(xy.at[0], xy.at[k], y_dev[k]) for k in far_first(ny)]
    prior0 = prior_part(rows0)
    for k in far_first(ny):
        bulk[k].wait_recv()
        build_points(k)
    hops0 = partial(0, prior0)
    rows1 = batch_rows(1)
    hops0 = stage_z(0, hops0)
    hops1 = partial(1, prior_part(rows1))
    vel0 = stage_end(0, hops0)
    vy[0] = vel0
    hop_vy = {k: send(vy.at[0], vy.at[k], y_dev[k]) for k in far_first(ny)}
    vg[s] = vel0
    hop_g = [send(vy.at[0], vg.at[s], s_dev[j]) for j in s_order]
    hops1 = stage_z(1, hops1)
    for copy in hop_xy:
        copy.wait_recv()
    xa1 = xa[1]
    for k in range(ny):
        block = xy[k]
        pa0[k, 0:32, :] = block
        pa0[k, 32:48, :] = extra_rows(split_norm(block), TILE, 3)
        kc[k] = jnp.exp(dot00(pa0[k], xa1)).astype(BF16)
    for copy in hop_g:
        copy.wait_recv()
    new0 = vg[...].reshape(64, TILE)
    mine, low = owned(0)
    for h in range(2):
        lanes = slice(h * TILE, (h + 1) * TILE)
        here = mine & (low == (h == 0))
        ov[:, lanes] = jnp.where(here, new0, vT[:, lanes])
        ou[:, lanes] = jnp.where(here, uT[:, lanes] + new0, uT[:, lanes])
    base1 = stage_end(1, hops1)

    corr = dot10(vy[0].astype(BF16), kc[0])
    for k in far_first(ny):
        hop_vy[k].wait_recv()
        corr = corr + dot10(vy[k].astype(BF16), kc[k])
    corr = corr * kv_scale
    cs[...] = corr[:, :TILE] + base1
    co[...] = corr[:, TILE:]
    fin[s] = cs[...]
    last = [send(co, cr.at[s], p_dev[j]) for j in s_order + [0]]
    last += [send(cs, fin.at[s], s_dev[j]) for j in s_order]
    for copy in last:
        copy.wait_recv()
    mine, low = owned(1)
    new1 = (fin[...] + cr[...]).reshape(64, TILE) + momentum * pick(ov, low)
    for h in range(2):
        lanes = slice(h * TILE, (h + 1) * TILE)
        here = mine & (low == (h == 0))
        before_v = ov[:, lanes]
        before_u = ou[:, lanes]
        ov[:, lanes] = jnp.where(here, new1, before_v)
        ou[:, lanes] = jnp.where(here, before_u + new1, before_u)
    for copy in started:
        copy.wait_send()


def local(
    nx, ny, nz,
    points, dual_weights, velocity, observed, noise_draws, frequencies, phases,
    prior_weights, batch_tiles,
):
    own, samples = dual_weights.shape
    feats = phases.shape[0]
    ns = nx * 2
    copies = 3 * (ny - 1) + 7 * (ns - 1) + 1 + 4 * (nz - 1)
    vm = pltpu.VMEM
    share = samples // ns
    out = jax.ShapeDtypeStruct((samples, own), F32)
    new_u, new_v = pl.pallas_call(
        functools.partial(
            kernel, nx, ny, nz, own * nx * ny * nz * 2, feats * nx * nz
        ),
        out_shape=(out, out),
        in_specs=[pl.BlockSpec(memory_space=pltpu.SMEM)]
        + [pl.BlockSpec(memory_space=pltpu.VMEM)] * 8,
        out_specs=(pl.BlockSpec(memory_space=pltpu.VMEM),) * 2,
        scratch_shapes=[
            vm((ny, 32 + samples, own), BF16),
            vm((ny, 48, own), BF16),
            vm((STEPS, 32, TILE), BF16),
            vm((ns, STEPS, 32, TILE), BF16),
            vm((STEPS, 32, TILE), BF16),
            vm((nz, STEPS, 32, TILE), BF16),
            vm((STEPS, 48, 2 * TILE), BF16),
            vm((ny, 32, TILE), BF16),
            vm((ny, 48, TILE), BF16),
            vm((ny, TILE, 2 * TILE), BF16),
            vm((STEPS, ns, share, 2 * TILE), F32),
            vm((STEPS, ns, share, 2 * TILE), F32),
            vm((STEPS, 2, share, TILE), F32),
            vm((STEPS, nz, share, TILE), F32),
            vm((ns, share, TILE), F32),
            vm((ny, share, TILE), F32),
            vm((share, TILE), F32),
            vm((share, TILE), F32),
            vm((ns, share, TILE), F32),
            vm((ns, share, TILE), F32),
            pltpu.SemaphoreType.DMA((copies,)),
            pltpu.SemaphoreType.DMA((copies,)),
        ],
        compiler_params=pltpu.CompilerParams(collective_id=0, has_side_effects=True),
    )(
        batch_tiles.reshape(STEPS),
        points.T,
        dual_weights.T,
        velocity.T,
        observed.reshape(1, own),
        noise_draws.T,
        frequencies,
        phases.reshape(1, feats),
        prior_weights.T,
    )
    return new_u.T, new_v.T


def solution(mesh):
    nx = NX
    ny = mesh.shape["grp"] // 2
    nz = mesh.shape["feat"] // nx
    return jax.shard_map(
        functools.partial(local, nx, ny, nz),
        mesh=mesh,
        in_specs=(
            P(("grp", "feat"), None),
            P(("grp", "feat"), None),
            P(("grp", "feat"), None),
            P(("grp", "feat")),
            P(("grp", "feat"), None),
            P(None, "feat"),
            P("feat"),
            P("feat", None),
            P(None, "grp", None),
        ),
        out_specs=(P(("grp", "feat"), None), P(("grp", "feat"), None)),
        check_vma=False,
    )
```

time: 987 us -> 50.5 us (0.05)
  waiting for transfers between devices: 730 us -> 0 us
  blocking collectives: 201 us -> 0 us
  Pallas kernels: 0 us -> 47.5 us
  local copies, waits for them, and re-layouts: 27.9 us -> 2.14 us
  between operations: 19.2 us -> 0.65 us
    psum x3 -> x0, waiting for transfers between devices: 730 us -> none  [the longest x2 539 us: local(): summed = lax.psum(partial_sums, ('grp', 'feat'))]
    psum x1 -> x0, blocking collectives: 144 us -> none  [local(): lax.psum(masked_rows(points, offsets, owned_mask).astype(jnp.bfloat16), '...]
    all_gather x2 -> x0, blocking collectives: 57.1 us -> none  [local(): lax.all_gather(batch_local, 'grp', axis=0, tiled=True)]
    pallas_call x0 -> x1, Pallas kernels: none -> 47.5 us  [local(): pl.pallas_call(functools.partial(kernel, nx, ny, nz, own * nx * ny * nz *...]
  transfers between devices with their start and end apart: 3 -> 0, of which waited for: 3 -> 0; matrix products, arithmetic and copies ran while one was open for 2% -> 0% of each run, Pallas kernels for 0% -> 0%
where the time goes in v1:
time: 50.5 us; the launch traced here: 50.3 us
  Pallas kernels  47.5 us (94%)
  local copies, waits for them, and re-layouts  2.14 us (4%)
  between operations  0.65 us (1%)
    pallas_call x1, Pallas kernels, local(): pl.pallas_call(functools.partial(kernel, nx, ny, nz, own * nx * ny * nz *...  47.5 us
    unnamed x4, local copies, waits for them, and re-layouts  2.14 us

profile of v1, /device:TPU:1, one launch (start us, length us, event | category | flops | bytes accessed | tf_op | source)
XLA Modules:
  0.0 50.3 jit_solution(14014344576072373761)
XLA Ops:
  0.6 47.5 %shard_map.104 = (f32[64,256]{1,0:T(8,128)}, f32[64,256]{1,0:T(8,128)}) custom-call(s32[2]{0:T(128)} %bitcast.19, bf16[32,256]{1,0:T(8,128)(2,1)} %bitcast.16, f32[64,256]{1,0:T(8,128)} %bitcast.10, f32[64,256]{1,0:T(8,128)} %bitcast.11, f32[1,256]{1,0:T(1,128)} %bitcast.18, f32[64,256]{1,0:T(8,128)} %bitcast.12, bf16[32,512]{1,0:T(8,128)(2,1)} %fr.1, ...), custom_call_target="tpu_custom_call" | custom-call | tf_op jit(solution)/shard_map/pallas_call | solution.py:294
  48.2 0.0 copy-start
  48.2 1.5 %copy.13 = f32[256,64]{0,1:T(8,128)} copy(f32[256,64]{0,1:T(8,128)} %bitcast.15) | data formatting | bytes 131072
  49.7 0.0 copy-done
  49.7 0.6 %copy.14 = f32[256,64]{0,1:T(8,128)} copy(f32[256,64]{0,1:T(8,128)S(1)} %bitcast.14) | data formatting | bytes 131072
Async XLA Ops:
  48.2 1.5 %copy-start = (f32[64,256]{1,0:T(8,128)S(1)}, f32[64,256]{1,0:T(8,128)}, u32[]{:S(2)}) copy-start(f32[64,256]{1,0:T(8,128)} %get-tuple-element.5) | copy-start | bytes 196612

commit v2 on v1

--- a/solution.py
+++ b/solution.py
@@ -69,13 +69,22 @@
 
 def kernel(
     nx, ny, nz, total_points, total_feats,
-    bt, pT, uT, vT, ob, nT, fr, ph, wT,
-    ou, ov,
+    bt_in, pT_in, uT_in, vT_in, ob_in, nT_in, fr_in, ph_in, wT_in,
+    du, dv,
+    bt, uT, vT, ob, nT, fr, ph, wT,
     gat, pa, xs1, xr1, xs2, xr2, xa, xy, pa0, kc,
-    pf, pr, zs, zr, vg, vy, cs, co, fin, cr, ssem, rsem,
+    pf, pr, zs, zr, vg, vy, cs, co, fin, cr, isem, ssem, rsem,
 ):
     nh = nz // 2
     ns = nx * 2
+    loads = []
+    for i, (src, dst) in enumerate((
+        (bt_in, bt), (pT_in, gat.at[0, pl.ds(0, 32)]), (uT_in, uT), (fr_in, fr), (ph_in, ph),
+        (wT_in, wT), (ob_in, ob), (nT_in, nT), (vT_in, vT),
+    )):
+        loads.append(pltpu.make_async_copy(src, dst, isem.at[i]))
+        loads[-1].start()
+
     g = lax.axis_index("grp")
     f = lax.axis_index("feat")
     y = lax.div(g, 2)
@@ -105,22 +114,28 @@
     z_dev = {k: at(s, y, lax.rem(z + k, nz)) for k in range(1, nz)}
 
     barrier = pltpu.get_barrier_semaphore()
-    greeted = list(s_dev.values()) + list(y_dev.values()) + list(z_dev.values())
-    greeted += [p_dev[j] for j in block_of]
+    greeted = [z_dev[k] for k in far_first(nz)] + [y_dev[k] for k in far_first(ny)]
+    greeted += [p_dev[j] for j in s_order] + [s_dev[j] for j in s_order]
     for d in greeted:
         pl.semaphore_signal(barrier, inc=1, device_id=d, device_id_type=MESH)
 
-    started = []
-
-    def send(src, dst, dev):
-        i = len(started)
-        copy = pltpu.make_async_remote_copy(
-            src_ref=src, dst_ref=dst, send_sem=ssem.at[i], recv_sem=rsem.at[i],
-            device_id=dev, device_id_type=MESH,
+    counts = [0, 0]
+    closing = []
+
+    def stage(copies, landing):
+        i = counts[0]
+        counts[0] += 1
+        for src, dst, dev in copies:
+            pltpu.make_async_remote_copy(
+                src_ref=src, dst_ref=dst, send_sem=ssem.at[i], recv_sem=rsem.at[i],
+                device_id=dev, device_id_type=MESH,
+            ).start()
+        whole = pltpu.make_async_remote_copy(
+            src_ref=landing, dst_ref=landing, send_sem=ssem.at[i], recv_sem=rsem.at[i],
+            device_id=copies[0][2], device_id_type=MESH,
         )
-        copy.start()
-        started.append(copy)
-        return copy
+        closing.append(whole)
+        return whole
 
     def owned(t):
         tile = bt[t]
@@ -129,24 +144,33 @@
     def pick(ref, low):
         return jnp.where(low, ref[:, :TILE], ref[:, TILE:])
 
-    gat[0, 0:32, :] = pT[...]
-    gat[0, 32:96, :] = uT[...].astype(BF16)
+    loads[0].wait()
+    loads[1].wait()
     for t in range(STEPS):
         mine, low = owned(t)
-        xs1[t] = jnp.where(mine, pick(pT, low).astype(F32), 0.0).astype(BF16)
+        tile_rows = jnp.where(low, gat[0, 0:32, 0:TILE], gat[0, 0:32, TILE:])
+        xs1[t] = jnp.where(mine, tile_rows.astype(F32), 0.0).astype(BF16)
     pl.semaphore_wait(barrier, len(greeted))
 
-    hop_c = [[send(xs1.at[t], xr1.at[j, t], s_dev[j]) for j in s_order] for t in range(STEPS)]
-    bulk = {k: send(gat.at[0], gat.at[k], y_dev[k]) for k in far_first(ny)}
+    hop_c = [
+        stage([(xs1.at[t], xr1.at[t, j], s_dev[j]) for j in s_order], xr1.at[t, pl.ds(1, ns - 1)])
+        for t in range(STEPS)
+    ]
+    loads[2].wait()
+    gat[0, 32:96, :] = uT[...].astype(BF16)
+    bulk = stage([(gat.at[0], gat.at[k], y_dev[k]) for k in far_first(ny)], gat.at[pl.ds(1, ny - 1)])
     hop_d = []
     for t in range(STEPS):
-        for copy in hop_c[t]:
-            copy.wait_recv()
+        hop_c[t].wait_recv()
         acc = xs1[t]
         for j in range(1, ns):
-            acc = acc + xr1[j, t]
+            acc = acc + xr1[t, j]
         xs2[t] = acc
-        hop_d.append([send(xs2.at[t], xr2.at[k, t], z_dev[k]) for k in far_first(nz)])
+        hop_d.append(stage(
+            [(xs2.at[t], xr2.at[t, k], z_dev[k]) for k in far_first(nz)], xr2.at[t, pl.ds(1, nz - 1)]
+        ))
+    for load in loads[3:]:
+        load.wait()
 
     def build_points(k):
         block = gat[k, 0:32, :]
@@ -154,14 +178,13 @@
         pa[k, 32:48, :] = extra_rows(split_norm(block), 2 * TILE, 3)
 
     def batch_rows(t):
-        for copy in hop_d[t]:
-            copy.wait_recv()
+        hop_d[t].wait_recv()
         own = xs2[t]
         for k in range(2, nz, 2):
-            own = own + xr2[k, t]
-        oth = xr2[1, t]
+            own = own + xr2[t, k]
+        oth = xr2[t, 1]
         for k in range(3, nz, 2):
-            oth = oth + xr2[k, t]
+            oth = oth + xr2[t, k]
         if t == 0:
             xy[0] = own
         for i, rows in enumerate((own, oth)):
@@ -195,88 +218,93 @@
 
     def partial(t, prior):
         part = kernel_part(t)
-        own = part[:, :TILE] + prior + own_terms(t)
+        own = part[:, :TILE] + prior
         pf[t, :, :, 0:TILE] = own.reshape(ns, 64 // ns, TILE)
         pf[t, :, :, TILE:] = part[:, TILE:].reshape(ns, 64 // ns, TILE)
-        return [send(pf.at[t, block_of[j]], pr.at[t, j], s_dev[j]) for j in s_order]
-
-    def stage_z(t, hops):
-        for copy in hops:
-            copy.wait_recv()
+        return stage(
+            [(pf.at[t, block_of[j]], pr.at[t, j], s_dev[j]) for j in s_order],
+            pr.at[t, pl.ds(1, ns - 1)],
+        )
+
+    def stage_z(t, hop):
+        hop.wait_recv()
         share = pf[t, s]
         for j in range(1, ns):
             share = share + pr[t, j]
         zs[t, 0] = share[:, :TILE]
         zs[t, 1] = share[:, TILE:]
-        return [send(zs.at[t, k % 2], zr.at[t, k], z_dev[k]) for k in far_first(nz)]
-
-    def stage_end(t, hops):
-        for copy in hops:
-            copy.wait_recv()
+        return stage(
+            [(zs.at[t, k % 2], zr.at[t, k], z_dev[k]) for k in far_first(nz)],
+            zr.at[t, pl.ds(1, nz - 1)],
+        )
+
+    def stage_end(t, hop):
+        hop.wait_recv()
         share = zs[t, 0]
         for k in range(1, nz):
             share = share + zr[t, k]
         return share
 
     build_points(0)
+    base0 = own_terms(0)
     rows0 = batch_rows(0)
-    hop_xy = [send(xy.at[0], xy.at[k], y_dev[k]) for k in far_first(ny)]
-    prior0 = prior_part(rows0)
-    for k in far_first(ny):
-        bulk[k].wait_recv()
+    hop_xy = stage([(xy.at[0], xy.at[k], y_dev[k]) for k in far_first(ny)], xy.at[pl.ds(1, ny - 1)])
+    prior0 = prior_part(rows0) + base0
+    bulk.wait_recv()
+    for k in range(1, ny):
         build_points(k)
-    hops0 = partial(0, prior0)
+    hop0 = partial(0, prior0)
+    base1 = own_terms(1)
     rows1 = batch_rows(1)
-    hops0 = stage_z(0, hops0)
-    hops1 = partial(1, prior_part(rows1))
-    vel0 = stage_end(0, hops0)
+    hop0 = stage_z(0, hop0)
+    hop1 = partial(1, prior_part(rows1) + base1)
+    vel0 = stage_end(0, hop0)
     vy[0] = vel0
-    hop_vy = {k: send(vy.at[0], vy.at[k], y_dev[k]) for k in far_first(ny)}
+    hop_vy = stage([(vy.at[0], vy.at[k], y_dev[k]) for k in far_first(ny)], vy.at[pl.ds(1, ny - 1)])
     vg[s] = vel0
-    hop_g = [send(vy.at[0], vg.at[s], s_dev[j]) for j in s_order]
-    hops1 = stage_z(1, hops1)
-    for copy in hop_xy:
-        copy.wait_recv()
+    hop_g = stage([(vy.at[0], vg.at[s], s_dev[j]) for j in s_order], vg.at[pl.ds(1, ns - 1)])
+    hop1 = stage_z(1, hop1)
+    hop_xy.wait_recv()
     xa1 = xa[1]
     for k in range(ny):
         block = xy[k]
         pa0[k, 0:32, :] = block
         pa0[k, 32:48, :] = extra_rows(split_norm(block), TILE, 3)
         kc[k] = jnp.exp(dot00(pa0[k], xa1)).astype(BF16)
-    for copy in hop_g:
-        copy.wait_recv()
+    hop_g.wait_recv()
     new0 = vg[...].reshape(64, TILE)
     mine, low = owned(0)
     for h in range(2):
         lanes = slice(h * TILE, (h + 1) * TILE)
         here = mine & (low == (h == 0))
-        ov[:, lanes] = jnp.where(here, new0, vT[:, lanes])
-        ou[:, lanes] = jnp.where(here, uT[:, lanes] + new0, uT[:, lanes])
-    base1 = stage_end(1, hops1)
-
+        du[:, lanes] = jnp.where(here, new0, 0.0)
+        dv[:, lanes] = jnp.where(here, new0 - vT[:, lanes], 0.0)
+    share1 = stage_end(1, hop1)
+    mine, low = owned(1)
+    kept = momentum * (pick(vT, low) + pick(dv, low))
+
+    hop_vy.wait_recv()
     corr = dot10(vy[0].astype(BF16), kc[0])
-    for k in far_first(ny):
-        hop_vy[k].wait_recv()
+    for k in range(1, ny):
         corr = corr + dot10(vy[k].astype(BF16), kc[k])
     corr = corr * kv_scale
-    cs[...] = corr[:, :TILE] + base1
+    cs[...] = corr[:, :TILE] + share1
     co[...] = corr[:, TILE:]
     fin[s] = cs[...]
-    last = [send(co, cr.at[s], p_dev[j]) for j in s_order + [0]]
-    last += [send(cs, fin.at[s], s_dev[j]) for j in s_order]
-    for copy in last:
-        copy.wait_recv()
-    mine, low = owned(1)
-    new1 = (fin[...] + cr[...]).reshape(64, TILE) + momentum * pick(ov, low)
+    last = stage([(co, cr.at[s], p_dev[j]) for j in s_order + [0]], cr)
+    last_s = stage([(cs, fin.at[s], s_dev[j]) for j in s_order], fin.at[pl.ds(1, ns - 1)])
+    for whole in closing[:-2]:
+        whole.wait_send()
+    last.wait_recv()
+    last_s.wait_recv()
+    new1 = (fin[...] + cr[...]).reshape(64, TILE) + kept
     for h in range(2):
         lanes = slice(h * TILE, (h + 1) * TILE)
         here = mine & (low == (h == 0))
-        before_v = ov[:, lanes]
-        before_u = ou[:, lanes]
-        ov[:, lanes] = jnp.where(here, new1, before_v)
-        ou[:, lanes] = jnp.where(here, before_u + new1, before_u)
-    for copy in started:
-        copy.wait_send()
+        du[:, lanes] = du[:, lanes] + jnp.where(here, new1, 0.0)
+        dv[:, lanes] = jnp.where(here, new1 - vT[:, lanes], dv[:, lanes])
+    last.wait_send()
+    last_s.wait_send()
 
 
 def local(
@@ -287,25 +315,32 @@
     own, samples = dual_weights.shape
     feats = phases.shape[0]
     ns = nx * 2
-    copies = 3 * (ny - 1) + 7 * (ns - 1) + 1 + 4 * (nz - 1)
+    stages = 14
     vm = pltpu.VMEM
     share = samples // ns
     out = jax.ShapeDtypeStruct((samples, own), F32)
-    new_u, new_v = pl.pallas_call(
+    add_u, add_v = pl.pallas_call(
         functools.partial(
             kernel, nx, ny, nz, own * nx * ny * nz * 2, feats * nx * nz
         ),
         out_shape=(out, out),
-        in_specs=[pl.BlockSpec(memory_space=pltpu.SMEM)]
-        + [pl.BlockSpec(memory_space=pltpu.VMEM)] * 8,
+        in_specs=[pl.BlockSpec(memory_space=pl.ANY)] * 9,
         out_specs=(pl.BlockSpec(memory_space=pltpu.VMEM),) * 2,
         scratch_shapes=[
+            pltpu.SMEM((STEPS,), jnp.int32),
+            vm((samples, own), F32),
+            vm((samples, own), F32),
+            vm((1, own), F32),
+            vm((samples, own), F32),
+            vm((32, feats), BF16),
+            vm((1, feats), F32),
+            vm((samples, feats), BF16),
             vm((ny, 32 + samples, own), BF16),
             vm((ny, 48, own), BF16),
             vm((STEPS, 32, TILE), BF16),
-            vm((ns, STEPS, 32, TILE), BF16),
+            vm((STEPS, ns, 32, TILE), BF16),
             vm((STEPS, 32, TILE), BF16),
-            vm((nz, STEPS, 32, TILE), BF16),
+            vm((STEPS, nz, 32, TILE), BF16),
             vm((STEPS, 48, 2 * TILE), BF16),
             vm((ny, 32, TILE), BF16),
             vm((ny, 48, TILE), BF16),
@@ -320,8 +355,9 @@
             vm((share, TILE), F32),
             vm((ns, share, TILE), F32),
             vm((ns, share, TILE), F32),
-            pltpu.SemaphoreType.DMA((copies,)),
-            pltpu.SemaphoreType.DMA((copies,)),
+            pltpu.SemaphoreType.DMA((9,)),
+            pltpu.SemaphoreType.DMA((stages,)),
+            pltpu.SemaphoreType.DMA((stages,)),
         ],
         compiler_params=pltpu.CompilerParams(collective_id=0, has_side_effects=True),
     )(
@@ -335,7 +371,7 @@
         phases.reshape(1, feats),
         prior_weights.T,
     )
-    return new_u.T, new_v.T
+    return dual_weights + add_u.T, velocity + add_v.T
 
 
 def solution(mesh):

time: 50.5 us -> 47.4 us (0.939)
  Pallas kernels: 47.5 us -> 45 us
  local copies, waits for them, and re-layouts: 2.14 us -> 0.01 us
  other arithmetic: 0 us -> 1.53 us
    pallas_call x1, Pallas kernels: 47.5 us -> 45 us  [local(): pl.pallas_call(functools.partial(kernel, nx, ny, nz, own * nx * ny * nz *...]
    unnamed x4, local copies, waits for them, and re-layouts: 2.14 us -> 0.01 us
    add x0 -> x1, other arithmetic: none -> 1.53 us  [local(): return (dual_weights + add_u.T, velocity + add_v.T)]
where the time goes in v2:
time: 47.4 us; the launch traced here: 47.2 us
  Pallas kernels  45 us (95%)
  other arithmetic  1.53 us (3%)
  between operations  0.67 us (1%)
    pallas_call x1, Pallas kernels, local(): pl.pallas_call(functools.partial(kernel, nx, ny, nz, own * nx * ny * nz *...  45 us
    add x1, other arithmetic, local(): return (dual_weights + add_u.T, velocity + add_v.T)  1.53 us

profile of v2, /device:TPU:1, one launch (start us, length us, event | category | flops | bytes accessed | tf_op | source)
XLA Modules:
  0.0 47.2 jit_solution(2873388074023050584)
XLA Ops:
  0.6 0.0 copy-start
  0.6 0.0 copy-start.1
  0.7 45.0 %shard_map.104 = (f32[64,256]{1,0:T(8,128)}, f32[64,256]{1,0:T(8,128)}) custom-call(s32[2]{0:T(128)} %bitcast.19, bf16[32,256]{1,0:T(8,128)(2,1)} %bitcast.16, f32[64,256]{1,0:T(8,128)} %bitcast.13, f32[64,256]{1,0:T(8,128)} %bitcast.12, f32[1,256]{1,0:T(1,128)} %bitcast.18, f32[64,256]{1,0:T(8,128)} %bitcast.14, bf16[32,512]{1,0:T(8,128)(2,1)} %fr_in.1, ...), custom_call_target="tpu_custom_call" | custom-call | tf_op jit(solution)/shard_map/pallas_call | solution.py:322
  45.7 0.0 copy-done
  45.7 0.0 copy-done.1
  45.7 1.5 %bitcast_add_fusion = (f32[256,64]{0,1:T(8,128)}, f32[256,64]{0,1:T(8,128)}) fusion(f32[256,64]{0,1:T(8,128)S(1)} %copy-done, f32[64,256]{1,0:T(8,128)} %get-tuple-element.5, f32[256,64]{0,1:T(8,128)S(1)} %copy-done.1, f32[64,256]{1,0:T(8,128)} %get-tuple-element.4), kind=kLoop, calls=%fused_computation | loop fusion | flops 32768 | bytes 393216 | tf_op jit(solution)/shard_map/add | solution.py:374
Async XLA Ops:
  0.6 45.0 %copy-start = (f32[256,64]{0,1:T(8,128)S(1)}, f32[256,64]{0,1:T(8,128)}, u32[]{:S(2)}) copy-start(f32[256,64]{0,1:T(8,128)} %param.11) | copy-start | bytes 196612
  0.6 45.0 %copy-start.1 = (f32[256,64]{0,1:T(8,128)S(1)}, f32[256,64]{0,1:T(8,128)}, u32[]{:S(2)}) copy-start(f32[256,64]{0,1:T(8,128)} %param.10) | copy-start | bytes 196612

commit v3 on v2

--- a/solution.py
+++ b/solution.py
@@ -318,7 +318,7 @@
     stages = 14
     vm = pltpu.VMEM
     share = samples // ns
-    out = jax.ShapeDtypeStruct((samples, own), F32)
+    out = vm((samples, own), F32)
     add_u, add_v = pl.pallas_call(
         functools.partial(
             kernel, nx, ny, nz, own * nx * ny * nz * 2, feats * nx * nz

time: 47.4 us -> 45.9 us (0.968)
  other arithmetic: 1.53 us -> 0.67 us
  Pallas kernels: 45 us -> 44.4 us
    add x1, other arithmetic: 1.53 us -> 0.67 us  [local(): return (dual_weights + add_u.T, velocity + add_v.T)]
    pallas_call x1, Pallas kernels: 45 us -> 44.4 us  [local(): pl.pallas_call(functools.partial(kernel, nx, ny, nz, own * nx * ny * nz *...]
where the time goes in v3:
time: 45.9 us; the launch traced here: 45.7 us
  Pallas kernels  44.4 us (97%)
  other arithmetic  0.67 us (1%)
  between operations  0.67 us (1%)
    pallas_call x1, Pallas kernels, local(): pl.pallas_call(functools.partial(kernel, nx, ny, nz, own * nx * ny * nz *...  44.4 us

profile of v3, /device:TPU:1, one launch (start us, length us, event | category | flops | bytes accessed | tf_op | source)
XLA Modules:
  0.0 45.7 jit_solution(2767806264116814630)
XLA Ops:
  0.6 0.0 copy-start
  0.6 0.0 copy-start.1
  0.7 44.4 %shard_map.104 = (f32[64,256]{1,0:T(8,128)S(1)}, f32[64,256]{1,0:T(8,128)S(1)}) custom-call(s32[2]{0:T(128)} %bitcast.19, bf16[32,256]{1,0:T(8,128)(2,1)} %bitcast.16, f32[64,256]{1,0:T(8,128)} %bitcast.13, f32[64,256]{1,0:T(8,128)} %bitcast.12, f32[1,256]{1,0:T(1,128)} %bitcast.18, f32[64,256]{1,0:T(8,128)} %bitcast.14, bf16[32,512]{1,0:T(8,128)(2,1)} %fr_in.1, ...), custom_call_target="tpu_custom_call" | custom-call | tf_op jit(solution)/shard_map/pallas_call | solution.py:322
  45.0 0.0 copy-done
  45.0 0.0 copy-done.1
  45.0 0.7 %bitcast_add_fusion = (f32[256,64]{0,1:T(8,128)}, f32[256,64]{0,1:T(8,128)}) fusion(f32[256,64]{0,1:T(8,128)S(1)} %copy-done, f32[64,256]{1,0:T(8,128)S(1)} %get-tuple-element.5, f32[256,64]{0,1:T(8,128)S(1)} %copy-done.1, f32[64,256]{1,0:T(8,128)S(1)} %get-tuple-element.4), kind=kLoop, calls=%fused_computation | loop fusion | flops 32768 | bytes 393216 | tf_op jit(solution)/shard_map/add | solution.py:374
Async XLA Ops:
  0.6 44.4 %copy-start = (f32[256,64]{0,1:T(8,128)S(1)}, f32[256,64]{0,1:T(8,128)}, u32[]{:S(2)}) copy-start(f32[256,64]{0,1:T(8,128)} %param.11) | copy-start | bytes 196612
  0.6 44.4 %copy-start.1 = (f32[256,64]{0,1:T(8,128)S(1)}, f32[256,64]{0,1:T(8,128)}, u32[]{:S(2)}) copy-start(f32[256,64]{0,1:T(8,128)} %param.10) | copy-start | bytes 196612

commit v4 on v3

--- a/solution.py
+++ b/solution.py
@@ -72,8 +72,8 @@
     bt_in, pT_in, uT_in, vT_in, ob_in, nT_in, fr_in, ph_in, wT_in,
     du, dv,
     bt, uT, vT, ob, nT, fr, ph, wT,
-    gat, pa, xs1, xr1, xs2, xr2, xa, xy, pa0, kc,
-    pf, pr, zs, zr, vg, vy, cs, co, fin, cr, isem, ssem, rsem,
+    gat, pa, xs1, xr1, xs2, xr2, xa, xy, pa0, kc, kk,
+    pf, pr, zs, zr, zb, vg, vy, cs, co, fin, isem, ssem, rsem,
 ):
     nh = nz // 2
     ns = nx * 2
@@ -106,16 +106,13 @@
 
     block_of = {j: lax.rem(s + j, ns) for j in range(1, ns)}
     s_order = sorted(range(1, ns), key=lambda j: (-min(j, ns - j), j))
-    z_flip = zh * 2 + (1 - zl)
     s_dev = {j: at(block_of[j], y, z) for j in block_of}
-    p_dev = {j: at(block_of[j], y, z_flip) for j in block_of}
-    p_dev[0] = at(s, y, z_flip)
     y_dev = {k: at(s, lax.rem(y + k, ny), z) for k in range(1, ny)}
     z_dev = {k: at(s, y, lax.rem(z + k, nz)) for k in range(1, nz)}
 
     barrier = pltpu.get_barrier_semaphore()
     greeted = [z_dev[k] for k in far_first(nz)] + [y_dev[k] for k in far_first(ny)]
-    greeted += [p_dev[j] for j in s_order] + [s_dev[j] for j in s_order]
+    greeted += [s_dev[j] for j in s_order]
     for d in greeted:
         pl.semaphore_signal(barrier, inc=1, device_id=d, device_id_type=MESH)
 
@@ -156,9 +153,16 @@
         stage([(xs1.at[t], xr1.at[t, j], s_dev[j]) for j in s_order], xr1.at[t, pl.ds(1, ns - 1)])
         for t in range(STEPS)
     ]
+    rows_p, rows_d = pl.ds(0, 32), pl.ds(32, 64)
+    others = pl.ds(1, ny - 1)
+    bulk = stage(
+        [(gat.at[0, rows_p], gat.at[k, rows_p], y_dev[k]) for k in far_first(ny)], gat.at[others, rows_p]
+    )
     loads[2].wait()
     gat[0, 32:96, :] = uT[...].astype(BF16)
-    bulk = stage([(gat.at[0], gat.at[k], y_dev[k]) for k in far_first(ny)], gat.at[pl.ds(1, ny - 1)])
+    bulk_d = stage(
+        [(gat.at[0, rows_d], gat.at[k, rows_d], y_dev[k]) for k in far_first(ny)], gat.at[others, rows_d]
+    )
     hop_d = []
     for t in range(STEPS):
         hop_c[t].wait_recv()
@@ -185,10 +189,10 @@
         oth = xr2[t, 1]
         for k in range(3, nz, 2):
             oth = oth + xr2[t, k]
-        if t == 0:
-            xy[0] = own
         for i, rows in enumerate((own, oth)):
             lanes = slice(i * TILE, (i + 1) * TILE)
+            if t == 0:
+                xy[0, :, lanes] = rows
             xa[t, 0:32, lanes] = (rows.astype(F32) * (2.0 / 32)).astype(BF16)
             xa[t, 32:48, lanes] = extra_rows(split_norm(rows), TILE, 0)
         return own
@@ -202,9 +206,13 @@
 
     def kernel_part(t):
         xat = xa[t]
+        if t == 0:
+            for k in range(ny):
+                kk[k] = jnp.exp(dot00(pa[k], xat)).astype(BF16)
+            bulk_d.wait_recv()
 
         def one(k, acc):
-            kern = jnp.exp(dot00(pa[k], xat)).astype(BF16)
+            kern = kk[k] if t == 0 else jnp.exp(dot00(pa[k], xat)).astype(BF16)
             return acc + dot10(gat[k, 32:96, :], kern)
 
         return lax.fori_loop(0, ny, one, jnp.zeros((64, 2 * TILE), F32), unroll=True) * kv_scale
@@ -231,46 +239,53 @@
         share = pf[t, s]
         for j in range(1, ns):
             share = share + pr[t, j]
-        zs[t, 0] = share[:, :TILE]
-        zs[t, 1] = share[:, TILE:]
+        if t == 0:
+            zb[0] = share
+            return stage(
+                [(zb.at[0], zb.at[k], z_dev[k]) for k in far_first(nz)], zb.at[pl.ds(1, nz - 1)]
+            )
+        zs[0] = share[:, :TILE]
+        zs[1] = share[:, TILE:]
         return stage(
-            [(zs.at[t, k % 2], zr.at[t, k], z_dev[k]) for k in far_first(nz)],
-            zr.at[t, pl.ds(1, nz - 1)],
+            [(zs.at[k % 2], zr.at[k], z_dev[k]) for k in far_first(nz)], zr.at[pl.ds(1, nz - 1)]
         )
 
     def stage_end(t, hop):
         hop.wait_recv()
-        share = zs[t, 0]
-        for k in range(1, nz):
-            share = share + zr[t, k]
-        return share
+        if t == 0:
+            even = sum((zb[k] for k in range(2, nz, 2)), zb[0])
+            odd = sum((zb[k] for k in range(3, nz, 2)), zb[1])
+            return even[:, :TILE] + odd[:, TILE:], even[:, TILE:] + odd[:, :TILE]
+        return sum((zr[k] for k in range(1, nz)), zs[0])
 
     build_points(0)
     base0 = own_terms(0)
-    rows0 = batch_rows(0)
-    hop_xy = stage([(xy.at[0], xy.at[k], y_dev[k]) for k in far_first(ny)], xy.at[pl.ds(1, ny - 1)])
-    prior0 = prior_part(rows0) + base0
     bulk.wait_recv()
     for k in range(1, ny):
         build_points(k)
+    rows0 = batch_rows(0)
+    prior0 = prior_part(rows0) + base0
     hop0 = partial(0, prior0)
+    hop_xy = stage([(xy.at[0], xy.at[k], y_dev[k]) for k in far_first(ny)], xy.at[pl.ds(1, ny - 1)])
     base1 = own_terms(1)
     rows1 = batch_rows(1)
+    hop1 = partial(1, prior_part(rows1) + base1)
     hop0 = stage_z(0, hop0)
-    hop1 = partial(1, prior_part(rows1) + base1)
-    vel0 = stage_end(0, hop0)
-    vy[0] = vel0
-    hop_vy = stage([(vy.at[0], vy.at[k], y_dev[k]) for k in far_first(ny)], vy.at[pl.ds(1, ny - 1)])
-    vg[s] = vel0
-    hop_g = stage([(vy.at[0], vg.at[s], s_dev[j]) for j in s_order], vg.at[pl.ds(1, ns - 1)])
     hop1 = stage_z(1, hop1)
     hop_xy.wait_recv()
-    xa1 = xa[1]
+    xa1 = xa[1, :, 0:TILE]
     for k in range(ny):
         block = xy[k]
         pa0[k, 0:32, :] = block
-        pa0[k, 32:48, :] = extra_rows(split_norm(block), TILE, 3)
+        pa0[k, 32:48, :] = extra_rows(split_norm(block), 2 * TILE, 3)
         kc[k] = jnp.exp(dot00(pa0[k], xa1)).astype(BF16)
+    vel0, vel0_oth = stage_end(0, hop0)
+    vy[0, :, 0:TILE] = vel0.astype(BF16)
+    vy[0, :, TILE:] = vel0_oth.astype(BF16)
+    hop_vy = stage([(vy.at[0], vy.at[k], y_dev[k]) for k in far_first(ny)], vy.at[pl.ds(1, ny - 1)])
+    co[...] = vel0
+    vg[s] = vel0
+    hop_g = stage([(co, vg.at[s], s_dev[j]) for j in s_order], vg.at[pl.ds(1, ns - 1)])
     hop_g.wait_recv()
     new0 = vg[...].reshape(64, TILE)
     mine, low = owned(0)
@@ -284,27 +299,22 @@
     kept = momentum * (pick(vT, low) + pick(dv, low))
 
     hop_vy.wait_recv()
-    corr = dot10(vy[0].astype(BF16), kc[0])
+    corr = dot10(vy[0], kc[0])
     for k in range(1, ny):
-        corr = corr + dot10(vy[k].astype(BF16), kc[k])
-    corr = corr * kv_scale
-    cs[...] = corr[:, :TILE] + share1
-    co[...] = corr[:, TILE:]
+        corr = corr + dot10(vy[k], kc[k])
+    cs[...] = corr * kv_scale + share1
     fin[s] = cs[...]
-    last = stage([(co, cr.at[s], p_dev[j]) for j in s_order + [0]], cr)
-    last_s = stage([(cs, fin.at[s], s_dev[j]) for j in s_order], fin.at[pl.ds(1, ns - 1)])
-    for whole in closing[:-2]:
+    last = stage([(cs, fin.at[s], s_dev[j]) for j in s_order], fin.at[pl.ds(1, ns - 1)])
+    for whole in closing[:-1]:
         whole.wait_send()
     last.wait_recv()
-    last_s.wait_recv()
-    new1 = (fin[...] + cr[...]).reshape(64, TILE) + kept
+    new1 = fin[...].reshape(64, TILE) + kept
     for h in range(2):
         lanes = slice(h * TILE, (h + 1) * TILE)
         here = mine & (low == (h == 0))
         du[:, lanes] = du[:, lanes] + jnp.where(here, new1, 0.0)
         dv[:, lanes] = jnp.where(here, new1 - vT[:, lanes], dv[:, lanes])
     last.wait_send()
-    last_s.wait_send()
 
 
 def local(
@@ -342,18 +352,19 @@
             vm((STEPS, 32, TILE), BF16),
             vm((STEPS, nz, 32, TILE), BF16),
             vm((STEPS, 48, 2 * TILE), BF16),
-            vm((ny, 32, TILE), BF16),
-            vm((ny, 48, TILE), BF16),
-            vm((ny, TILE, 2 * TILE), BF16),
+            vm((ny, 32, 2 * TILE), BF16),
+            vm((ny, 48, 2 * TILE), BF16),
+            vm((ny, 2 * TILE, TILE), BF16),
+            vm((ny, own, 2 * TILE), BF16),
             vm((STEPS, ns, share, 2 * TILE), F32),
             vm((STEPS, ns, share, 2 * TILE), F32),
-            vm((STEPS, 2, share, TILE), F32),
-            vm((STEPS, nz, share, TILE), F32),
+            vm((2, share, TILE), F32),
+            vm((nz, share, TILE), F32),
+            vm((nz, share, 2 * TILE), F32),
             vm((ns, share, TILE), F32),
-            vm((ny, share, TILE), F32),
+            vm((ny, share, 2 * TILE), BF16),
             vm((share, TILE), F32),
             vm((share, TILE), F32),
-            vm((ns, share, TILE), F32),
             vm((ns, share, TILE), F32),
             pltpu.SemaphoreType.DMA((9,)),
             pltpu.SemaphoreType.DMA((stages,)),

time: 45.9 us -> 43.9 us (0.956)
  Pallas kernels: 44.4 us -> 42.4 us
    pallas_call x1, Pallas kernels: 44.4 us -> 42.4 us  [local(): pl.pallas_call(functools.partial(kernel, nx, ny, nz, own * nx * ny * nz *...]
where the time goes in v4:
time: 43.9 us; the launch traced here: 43.7 us
  Pallas kernels  42.4 us (97%)
  other arithmetic  0.67 us (2%)
  between operations  0.67 us (2%)
    pallas_call x1, Pallas kernels, local(): pl.pallas_call(functools.partial(kernel, nx, ny, nz, own * nx * ny * nz *...  42.4 us

profile of v4, /device:TPU:1, one launch (start us, length us, event | category | flops | bytes accessed | tf_op | source)
XLA Modules:
  0.0 43.7 jit_solution(13791991606268968228)
XLA Ops:
  0.6 0.0 copy-start
  0.6 0.0 copy-start.1
  0.7 42.4 %shard_map.104 = (f32[64,256]{1,0:T(8,128)S(1)}, f32[64,256]{1,0:T(8,128)S(1)}) custom-call(s32[2]{0:T(128)} %bitcast.19, bf16[32,256]{1,0:T(8,128)(2,1)} %bitcast.16, f32[64,256]{1,0:T(8,128)} %bitcast.13, f32[64,256]{1,0:T(8,128)} %bitcast.12, f32[1,256]{1,0:T(1,128)} %bitcast.18, f32[64,256]{1,0:T(8,128)} %bitcast.14, bf16[32,512]{1,0:T(8,128)(2,1)} %fr_in.1, ...), custom_call_target="tpu_custom_call" | custom-call | tf_op jit(solution)/shard_map/pallas_call | solution.py:332
  43.0 0.0 copy-done
  43.1 0.0 copy-done.1
  43.1 0.7 %bitcast_add_fusion = (f32[256,64]{0,1:T(8,128)}, f32[256,64]{0,1:T(8,128)}) fusion(f32[256,64]{0,1:T(8,128)S(1)} %copy-done, f32[64,256]{1,0:T(8,128)S(1)} %get-tuple-element.5, f32[256,64]{0,1:T(8,128)S(1)} %copy-done.1, f32[64,256]{1,0:T(8,128)S(1)} %get-tuple-element.4), kind=kLoop, calls=%fused_computation | loop fusion | flops 32768 | bytes 393216 | tf_op jit(solution)/shard_map/add | solution.py:385
Async XLA Ops:
  0.6 42.4 %copy-start = (f32[256,64]{0,1:T(8,128)S(1)}, f32[256,64]{0,1:T(8,128)}, u32[]{:S(2)}) copy-start(f32[256,64]{0,1:T(8,128)} %param.11) | copy-start | bytes 196612
  0.6 42.4 %copy-start.1 = (f32[256,64]{0,1:T(8,128)S(1)}, f32[256,64]{0,1:T(8,128)}, u32[]{:S(2)}) copy-start(f32[256,64]{0,1:T(8,128)} %param.10) | copy-start | bytes 196612

commit v5 on v4

--- a/solution.py
+++ b/solution.py
@@ -73,7 +73,7 @@
     du, dv,
     bt, uT, vT, ob, nT, fr, ph, wT,
     gat, pa, xs1, xr1, xs2, xr2, xa, xy, pa0, kc, kk,
-    pf, pr, zs, zr, zb, vg, vy, cs, co, fin, isem, ssem, rsem,
+    pf, pr, zs, zr, vg, vy, cs, sg, fz, isem, ssem, rsem,
 ):
     nh = nz // 2
     ns = nx * 2
@@ -239,24 +239,27 @@
         share = pf[t, s]
         for j in range(1, ns):
             share = share + pr[t, j]
+        hop = None
         if t == 0:
-            zb[0] = share
-            return stage(
-                [(zb.at[0], zb.at[k], z_dev[k]) for k in far_first(nz)], zb.at[pl.ds(1, nz - 1)]
-            )
-        zs[0] = share[:, :TILE]
-        zs[1] = share[:, TILE:]
-        return stage(
-            [(zs.at[k % 2], zr.at[k], z_dev[k]) for k in far_first(nz)], zr.at[pl.ds(1, nz - 1)]
+            vy[0] = share.astype(BF16)
+            hop = stage([(vy.at[0], vy.at[k], y_dev[k]) for k in far_first(ny)], vy.at[pl.ds(1, ny - 1)])
+        zs[t, 0] = share[:, :TILE]
+        zs[t, 1] = share[:, TILE:]
+        return hop, stage(
+            [(zs.at[t, k % 2], zr.at[t, k], z_dev[k]) for k in far_first(nz)],
+            zr.at[t, pl.ds(1, nz - 1)],
         )
 
     def stage_end(t, hop):
         hop.wait_recv()
-        if t == 0:
-            even = sum((zb[k] for k in range(2, nz, 2)), zb[0])
-            odd = sum((zb[k] for k in range(3, nz, 2)), zb[1])
-            return even[:, :TILE] + odd[:, TILE:], even[:, TILE:] + odd[:, :TILE]
-        return sum((zr[k] for k in range(1, nz)), zs[0])
+        return sum((zr[t, k] for k in range(1, nz)), zs[t, 0])
+
+    def gather_shares(t, share):
+        sg[t] = share
+        vg[t, s] = share
+        return stage(
+            [(sg.at[t], vg.at[t, s], s_dev[j]) for j in s_order], vg.at[t, pl.ds(1, ns - 1)]
+        )
 
     build_points(0)
     base0 = own_terms(0)
@@ -270,51 +273,55 @@
     base1 = own_terms(1)
     rows1 = batch_rows(1)
     hop1 = partial(1, prior_part(rows1) + base1)
-    hop0 = stage_z(0, hop0)
-    hop1 = stage_z(1, hop1)
+    hop_vy, hop0 = stage_z(0, hop0)
+    hop1 = stage_z(1, hop1)[1]
     hop_xy.wait_recv()
-    xa1 = xa[1, :, 0:TILE]
+    xa1 = xa[1]
     for k in range(ny):
         block = xy[k]
         pa0[k, 0:32, :] = block
         pa0[k, 32:48, :] = extra_rows(split_norm(block), 2 * TILE, 3)
         kc[k] = jnp.exp(dot00(pa0[k], xa1)).astype(BF16)
-    vel0, vel0_oth = stage_end(0, hop0)
-    vy[0, :, 0:TILE] = vel0.astype(BF16)
-    vy[0, :, TILE:] = vel0_oth.astype(BF16)
-    hop_vy = stage([(vy.at[0], vy.at[k], y_dev[k]) for k in far_first(ny)], vy.at[pl.ds(1, ny - 1)])
-    co[...] = vel0
-    vg[s] = vel0
-    hop_g = stage([(co, vg.at[s], s_dev[j]) for j in s_order], vg.at[pl.ds(1, ns - 1)])
-    hop_g.wait_recv()
-    new0 = vg[...].reshape(64, TILE)
+
+    hop_vy.wait_recv()
+    corr = dot10(vy[0], kc[0])
+    for k in range(1, ny):
+        corr = corr + dot10(vy[k], kc[k])
+    corr = (corr * kv_scale).astype(BF16)
+    cs[0] = corr[:, :TILE]
+    cs[1] = corr[:, TILE:]
+    fz[0, s] = corr[:, :TILE]
+    copies = [
+        (cs.at[k % 2], fz.at[k, s], at(s if j == 0 else block_of[j], y, lax.rem(z + k, nz)))
+        for k in far_first(nz) for j in s_order + [0]
+    ]
+    last = stage(copies, fz.at[pl.ds(1, nz - 1)])
+    last_s = stage([(cs.at[0], fz.at[0, s], s_dev[j]) for j in s_order], fz.at[0, pl.ds(1, ns - 1)])
+
+    hop_g0 = gather_shares(0, stage_end(0, hop0))
+    hop_g1 = gather_shares(1, stage_end(1, hop1))
+    hop_g0.wait_recv()
+    new0 = vg[0].reshape(64, TILE)
     mine, low = owned(0)
     for h in range(2):
         lanes = slice(h * TILE, (h + 1) * TILE)
         here = mine & (low == (h == 0))
         du[:, lanes] = jnp.where(here, new0, 0.0)
         dv[:, lanes] = jnp.where(here, new0 - vT[:, lanes], 0.0)
-    share1 = stage_end(1, hop1)
     mine, low = owned(1)
     kept = momentum * (pick(vT, low) + pick(dv, low))
-
-    hop_vy.wait_recv()
-    corr = dot10(vy[0], kc[0])
-    for k in range(1, ny):
-        corr = corr + dot10(vy[k], kc[k])
-    cs[...] = corr * kv_scale + share1
-    fin[s] = cs[...]
-    last = stage([(cs, fin.at[s], s_dev[j]) for j in s_order], fin.at[pl.ds(1, ns - 1)])
-    for whole in closing[:-1]:
+    hop_g1.wait_recv()
+    kept = kept + vg[1].reshape(64, TILE)
+    for whole in closing:
         whole.wait_send()
     last.wait_recv()
-    new1 = fin[...].reshape(64, TILE) + kept
+    last_s.wait_recv()
+    new1 = sum((fz[k].astype(F32) for k in range(1, nz)), fz[0].astype(F32)).reshape(64, TILE) + kept
     for h in range(2):
         lanes = slice(h * TILE, (h + 1) * TILE)
         here = mine & (low == (h == 0))
         du[:, lanes] = du[:, lanes] + jnp.where(here, new1, 0.0)
         dv[:, lanes] = jnp.where(here, new1 - vT[:, lanes], dv[:, lanes])
-    last.wait_send()
 
 
 def local(
@@ -325,7 +332,7 @@
     own, samples = dual_weights.shape
     feats = phases.shape[0]
     ns = nx * 2
-    stages = 14
+    stages = 16
     vm = pltpu.VMEM
     share = samples // ns
     out = vm((samples, own), F32)
@@ -354,18 +361,17 @@
             vm((STEPS, 48, 2 * TILE), BF16),
             vm((ny, 32, 2 * TILE), BF16),
             vm((ny, 48, 2 * TILE), BF16),
-            vm((ny, 2 * TILE, TILE), BF16),
+            vm((ny, 2 * TILE, 2 * TILE), BF16),
             vm((ny, own, 2 * TILE), BF16),
             vm((STEPS, ns, share, 2 * TILE), F32),
             vm((STEPS, ns, share, 2 * TILE), F32),
-            vm((2, share, TILE), F32),
-            vm((nz, share, TILE), F32),
-            vm((nz, share, 2 * TILE), F32),
-            vm((ns, share, TILE), F32),
+            vm((STEPS, 2, share, TILE), F32),
+            vm((STEPS, nz, share, TILE), F32),
+            vm((STEPS, ns, share, TILE), F32),
             vm((ny, share, 2 * TILE), BF16),
-            vm((share, TILE), F32),
-            vm((share, TILE), F32),
-            vm((ns, share, TILE), F32),
+            vm((2, share, TILE), BF16),
+            vm((STEPS, share, TILE), F32),
+            vm((nz, ns, share, TILE), BF16),
             pltpu.SemaphoreType.DMA((9,)),
             pltpu.SemaphoreType.DMA((stages,)),
             pltpu.SemaphoreType.DMA((stages,)),

time: 43.9 us -> 42.7 us (0.973)
  Pallas kernels: 42.4 us -> 41.2 us
    pallas_call x1, Pallas kernels: 42.4 us -> 41.2 us  [local(): pl.pallas_call(functools.partial(kernel, nx, ny, nz, own * nx * ny * nz *...]
where the time goes in v5:
time: 42.7 us; the launch traced here: 42.5 us
  Pallas kernels  41.2 us (96%)
  other arithmetic  0.67 us (2%)
  between operations  0.67 us (2%)
    pallas_call x1, Pallas kernels, local(): pl.pallas_call(functools.partial(kernel, nx, ny, nz, own * nx * ny * nz *...  41.2 us

profile of v5, /device:TPU:1, one launch (start us, length us, event | category | flops | bytes accessed | tf_op | source)
XLA Modules:
  0.0 42.5 jit_solution(114059382758839745)
XLA Ops:
  0.6 0.0 copy-start
  0.6 0.0 copy-start.1
  0.7 41.2 %shard_map.104 = (f32[64,256]{1,0:T(8,128)S(1)}, f32[64,256]{1,0:T(8,128)S(1)}) custom-call(s32[2]{0:T(128)} %bitcast.19, bf16[32,256]{1,0:T(8,128)(2,1)} %bitcast.16, f32[64,256]{1,0:T(8,128)} %bitcast.13, f32[64,256]{1,0:T(8,128)} %bitcast.12, f32[1,256]{1,0:T(1,128)} %bitcast.18, f32[64,256]{1,0:T(8,128)} %bitcast.14, bf16[32,512]{1,0:T(8,128)(2,1)} %fr_in.1, ...), custom_call_target="tpu_custom_call" | custom-call | tf_op jit(solution)/shard_map/pallas_call | solution.py:339
  41.8 0.0 copy-done
  41.9 0.0 copy-done.1
  41.9 0.7 %bitcast_add_fusion = (f32[256,64]{0,1:T(8,128)}, f32[256,64]{0,1:T(8,128)}) fusion(f32[256,64]{0,1:T(8,128)S(1)} %copy-done, f32[64,256]{1,0:T(8,128)S(1)} %get-tuple-element.5, f32[256,64]{0,1:T(8,128)S(1)} %copy-done.1, f32[64,256]{1,0:T(8,128)S(1)} %get-tuple-element.4), kind=kLoop, calls=%fused_computation | loop fusion | flops 32768 | bytes 393216 | tf_op jit(solution)/shard_map/add | solution.py:391
Async XLA Ops:
  0.6 41.2 %copy-start = (f32[256,64]{0,1:T(8,128)S(1)}, f32[256,64]{0,1:T(8,128)}, u32[]{:S(2)}) copy-start(f32[256,64]{0,1:T(8,128)} %param.11) | copy-start | bytes 196612
  0.6 41.2 %copy-start.1 = (f32[256,64]{0,1:T(8,128)S(1)}, f32[256,64]{0,1:T(8,128)}, u32[]{:S(2)}) copy-start(f32[256,64]{0,1:T(8,128)} %param.10) | copy-start | bytes 196612

commit v6 on v5

--- a/solution.py
+++ b/solution.py
@@ -207,12 +207,17 @@
     def kernel_part(t):
         xat = xa[t]
         if t == 0:
-            for k in range(ny):
+            for k in range(ny // 2):
                 kk[k] = jnp.exp(dot00(pa[k], xat)).astype(BF16)
             bulk_d.wait_recv()
+            acc = jnp.zeros((64, 2 * TILE), F32)
+            for k in range(ny):
+                kern = kk[k] if k < ny // 2 else jnp.exp(dot00(pa[k], xat)).astype(BF16)
+                acc = acc + dot10(gat[k, 32:96, :], kern)
+            return acc * kv_scale
 
         def one(k, acc):
-            kern = kk[k] if t == 0 else jnp.exp(dot00(pa[k], xat)).astype(BF16)
+            kern = jnp.exp(dot00(pa[k], xat)).astype(BF16)
             return acc + dot10(gat[k, 32:96, :], kern)
 
         return lax.fori_loop(0, ny, one, jnp.zeros((64, 2 * TILE), F32), unroll=True) * kv_scale
@@ -293,7 +298,7 @@
     fz[0, s] = corr[:, :TILE]
     copies = [
         (cs.at[k % 2], fz.at[k, s], at(s if j == 0 else block_of[j], y, lax.rem(z + k, nz)))
-        for k in far_first(nz) for j in s_order + [0]
+        for j in s_order + [0] for k in far_first(nz)
     ]
     last = stage(copies, fz.at[pl.ds(1, nz - 1)])
     last_s = stage([(cs.at[0], fz.at[0, s], s_dev[j]) for j in s_order], fz.at[0, pl.ds(1, ns - 1)])

time: 42.7 us -> 42.3 us (level)
  no operation moved by 1% of the time
where the time goes in v6:
time: 42.3 us; the launch traced here: 42.1 us
  Pallas kernels  40.8 us (96%)
  other arithmetic  0.67 us (2%)
  between operations  0.67 us (2%)
    pallas_call x1, Pallas kernels, local(): pl.pallas_call(functools.partial(kernel, nx, ny, nz, own * nx * ny * nz *...  40.8 us

profile of v6, /device:TPU:1, one launch (start us, length us, event | category | flops | bytes accessed | tf_op | source)
XLA Modules:
  0.0 42.1 jit_solution(5112930962416893521)
XLA Ops:
  0.6 0.0 copy-start
  0.6 0.0 copy-start.1
  0.7 40.8 %shard_map.104 = (f32[64,256]{1,0:T(8,128)S(1)}, f32[64,256]{1,0:T(8,128)S(1)}) custom-call(s32[2]{0:T(128)} %bitcast.19, bf16[32,256]{1,0:T(8,128)(2,1)} %bitcast.16, f32[64,256]{1,0:T(8,128)} %bitcast.13, f32[64,256]{1,0:T(8,128)} %bitcast.12, f32[1,256]{1,0:T(1,128)} %bitcast.18, f32[64,256]{1,0:T(8,128)} %bitcast.14, bf16[32,512]{1,0:T(8,128)(2,1)} %fr_in.1, ...), custom_call_target="tpu_custom_call" | custom-call | tf_op jit(solution)/shard_map/pallas_call | solution.py:344
  41.5 0.0 copy-done
  41.5 0.0 copy-done.1
  41.5 0.7 %bitcast_add_fusion = (f32[256,64]{0,1:T(8,128)}, f32[256,64]{0,1:T(8,128)}) fusion(f32[256,64]{0,1:T(8,128)S(1)} %copy-done, f32[64,256]{1,0:T(8,128)S(1)} %get-tuple-element.5, f32[256,64]{0,1:T(8,128)S(1)} %copy-done.1, f32[64,256]{1,0:T(8,128)S(1)} %get-tuple-element.4), kind=kLoop, calls=%fused_computation | loop fusion | flops 32768 | bytes 393216 | tf_op jit(solution)/shard_map/add | solution.py:396
Async XLA Ops:
  0.6 40.8 %copy-start = (f32[256,64]{0,1:T(8,128)S(1)}, f32[256,64]{0,1:T(8,128)}, u32[]{:S(2)}) copy-start(f32[256,64]{0,1:T(8,128)} %param.11) | copy-start | bytes 196612
  0.6 40.8 %copy-start.1 = (f32[256,64]{0,1:T(8,128)S(1)}, f32[256,64]{0,1:T(8,128)}, u32[]{:S(2)}) copy-start(f32[256,64]{0,1:T(8,128)} %param.10) | copy-start | bytes 196612

commit v7 on v6

--- a/solution.py
+++ b/solution.py
@@ -259,13 +259,6 @@
         hop.wait_recv()
         return sum((zr[t, k] for k in range(1, nz)), zs[t, 0])
 
-    def gather_shares(t, share):
-        sg[t] = share
-        vg[t, s] = share
-        return stage(
-            [(sg.at[t], vg.at[t, s], s_dev[j]) for j in s_order], vg.at[t, pl.ds(1, ns - 1)]
-        )
-
     build_points(0)
     base0 = own_terms(0)
     bulk.wait_recv()
@@ -303,10 +296,12 @@
     last = stage(copies, fz.at[pl.ds(1, nz - 1)])
     last_s = stage([(cs.at[0], fz.at[0, s], s_dev[j]) for j in s_order], fz.at[0, pl.ds(1, ns - 1)])
 
-    hop_g0 = gather_shares(0, stage_end(0, hop0))
-    hop_g1 = gather_shares(1, stage_end(1, hop1))
-    hop_g0.wait_recv()
-    new0 = vg[0].reshape(64, TILE)
+    for t, hop in enumerate((hop0, hop1)):
+        share = stage_end(t, hop)
+        sg[t] = share
+        vg[s, t] = share
+    stage([(sg, vg.at[s], s_dev[j]) for j in s_order], vg.at[pl.ds(1, ns - 1)]).wait_recv()
+    new0 = vg[:, 0].reshape(64, TILE)
     mine, low = owned(0)
     for h in range(2):
         lanes = slice(h * TILE, (h + 1) * TILE)
@@ -315,8 +310,7 @@
         dv[:, lanes] = jnp.where(here, new0 - vT[:, lanes], 0.0)
     mine, low = owned(1)
     kept = momentum * (pick(vT, low) + pick(dv, low))
-    hop_g1.wait_recv()
-    kept = kept + vg[1].reshape(64, TILE)
+    kept = kept + vg[:, 1].reshape(64, TILE)
     for whole in closing:
         whole.wait_send()
     last.wait_recv()
@@ -337,7 +331,7 @@
     own, samples = dual_weights.shape
     feats = phases.shape[0]
     ns = nx * 2
-    stages = 16
+    stages = 15
     vm = pltpu.VMEM
     share = samples // ns
     out = vm((samples, own), F32)
@@ -372,7 +366,7 @@
             vm((STEPS, ns, share, 2 * TILE), F32),
             vm((STEPS, 2, share, TILE), F32),
             vm((STEPS, nz, share, TILE), F32),
-            vm((STEPS, ns, share, TILE), F32),
+            vm((ns, STEPS, share, TILE), F32),
             vm((ny, share, 2 * TILE), BF16),
             vm((2, share, TILE), BF16),
             vm((STEPS, share, TILE), F32),

time: 42.3 us -> 42.3 us (level)
  no operation moved by 1% of the time
where the time goes in v7:
time: 42.3 us; the launch traced here: 42.1 us
  Pallas kernels  40.8 us (96%)
  other arithmetic  0.67 us (2%)
  between operations  0.67 us (2%)
    pallas_call x1, Pallas kernels, local(): pl.pallas_call(functools.partial(kernel, nx, ny, nz, own * nx * ny * nz *...  40.8 us

profile of v7, /device:TPU:1, one launch (start us, length us, event | category | flops | bytes accessed | tf_op | source)
XLA Modules:
  0.0 42.1 jit_solution(3068147006347731738)
XLA Ops:
  0.6 0.0 copy-start
  0.6 0.0 copy-start.1
  0.7 40.8 %shard_map.104 = (f32[64,256]{1,0:T(8,128)S(1)}, f32[64,256]{1,0:T(8,128)S(1)}) custom-call(s32[2]{0:T(128)} %bitcast.19, bf16[32,256]{1,0:T(8,128)(2,1)} %bitcast.16, f32[64,256]{1,0:T(8,128)} %bitcast.13, f32[64,256]{1,0:T(8,128)} %bitcast.12, f32[1,256]{1,0:T(1,128)} %bitcast.18, f32[64,256]{1,0:T(8,128)} %bitcast.14, bf16[32,512]{1,0:T(8,128)(2,1)} %fr_in.1, ...), custom_call_target="tpu_custom_call" | custom-call | tf_op jit(solution)/shard_map/pallas_call | solution.py:338
  41.4 0.0 copy-done
  41.4 0.0 copy-done.1
  41.5 0.7 %bitcast_add_fusion = (f32[256,64]{0,1:T(8,128)}, f32[256,64]{0,1:T(8,128)}) fusion(f32[256,64]{0,1:T(8,128)S(1)} %copy-done, f32[64,256]{1,0:T(8,128)S(1)} %get-tuple-element.5, f32[256,64]{0,1:T(8,128)S(1)} %copy-done.1, f32[64,256]{1,0:T(8,128)S(1)} %get-tuple-element.4), kind=kLoop, calls=%fused_computation | loop fusion | flops 32768 | bytes 393216 | tf_op jit(solution)/shard_map/add | solution.py:390
Async XLA Ops:
  0.6 40.8 %copy-start = (f32[256,64]{0,1:T(8,128)S(1)}, f32[256,64]{0,1:T(8,128)}, u32[]{:S(2)}) copy-start(f32[256,64]{0,1:T(8,128)} %param.11) | copy-start | bytes 196612
  0.6 40.8 %copy-start.1 = (f32[256,64]{0,1:T(8,128)S(1)}, f32[256,64]{0,1:T(8,128)}, u32[]{:S(2)}) copy-start(f32[256,64]{0,1:T(8,128)} %param.10) | copy-start | bytes 196612
